TPU v7x, 256 devices: a whole 4x4x8 slice. The times are simulated.
256 devices in a mesh: region: 32 (over y, z), sub: 8 (over x, core).
Axes of the slice: x: 4, y: 4, z: 8, core: 2. Of those that a mesh axis runs over, the one named last changes fastest.
Arguments:
- mode_rows: bfloat16 [131072, 4096], P(('region', 'sub')), may hold values from -0.09375 to 0.09375
- input_rows: bfloat16 [512, 4096], P(('region', 'sub')), may hold values from -0.25 to 0.25
- input_factor: bfloat16 [512, 128], P(('region', 'sub')), may hold values from -6 to 6
- mode_freq: float32 [4096], replicated, may hold values from 0.5 to 2
- mode_damping: float32 [4096], replicated, may hold values from 0.02 to 0.2
- line_freq: float32 [2], replicated, may hold values from 0.6 to 1.6
- boundary_rows: int32 [32768], P(('region', 'sub')), may hold values from 0 to 511
- connectivity: int32 [4, 131072], P(None, ('region', 'sub')), may hold values from 0 to 639
- stress_coef: float32 [4, 131072], P(None, ('region', 'sub')), may hold values from -3 to 3
Outputs:
- stress_psd: float32 [2, 131072], P(None, ('region', 'sub'))
Inputs may be any that keep to these rules, and one draw needn't show every extreme that they name: `boundary_rows`: local row numbers of the sending device. `connectivity`: rows of the node table of the element's device.
All inputs are finite; a program needn't handle non-finite values.
Results may differ from a plain program's by a relative error of at most 0.0013.
Values may be sent and summed in bfloat16 or wider, within the bound.
A program may use at most 64 MiB of HBM per device.

v0:
```python
import jax
import jax.numpy as jnp
from jax import lax
from jax.sharding import PartitionSpec as P


def extended(cells, sides, width):
    for axis, dim in sides:
        count = lax.axis_size(axis)
        ends = count - 1
        head = lax.slice_in_dim(cells, 0, width, axis=dim)
        tail = lax.slice_in_dim(cells, cells.shape[dim] - width, cells.shape[dim], axis=dim)
        cells = jnp.concatenate(
            [
                lax.ppermute(tail, axis, [(i, (i + 1) % count) for i in range(ends)]),
                cells,
                lax.ppermute(head, axis, [((i + 1) % count, i) for i in range(ends)]),
            ],
            axis=dim,
        )
    return cells


def modal_gain(mode_freq, mode_damping, line_omega):
    detune = mode_freq * mode_freq - line_omega * line_omega
    damped = 2.0 * mode_damping * mode_freq * line_omega
    magnitude = detune * detune + damped * damped
    return (detune / magnitude, -damped / magnitude)


def apply_gain(summed, gain_real, gain_imag):
    half_cols = summed.shape[1] // 2
    forced_real = summed[:, :half_cols]
    forced_imag = summed[:, half_cols:]
    out_real = gain_real[:, None] * forced_real - gain_imag[:, None] * forced_imag
    out_imag = gain_real[:, None] * forced_imag + gain_imag[:, None] * forced_real
    return jnp.concatenate([out_real, out_imag], axis=1).astype(jnp.bfloat16)


def scale_lines(summed, mode_freq, mode_damping, line_freq, columns):
    pieces = []
    for line_no in range(line_freq.shape[0]):
        gain_real, gain_imag = modal_gain(mode_freq, mode_damping, line_freq[line_no])
        pieces.append(
            apply_gain(summed[:, line_no * columns : (line_no + 1) * columns], gain_real, gain_imag)
        )
    return jnp.concatenate(pieces, axis=1)


def local(
    mode_rows,
    input_rows,
    input_factor,
    mode_freq,
    mode_damping,
    line_freq,
    boundary_rows,
    connectivity,
    stress_coef,
):
    mode_count = input_rows.shape[1]
    line_count = line_freq.shape[0]
    width_all = input_factor.shape[1]
    columns = width_all // line_count
    partial_value = lax.dot_general(
        input_rows, input_factor, (((0,), (0,)), ((), ())), preferred_element_type=jnp.float32
    )
    summed = lax.psum(
        partial_value.reshape(mode_count // 2, 2 * width_all), ("region", "sub")
    ).reshape(mode_count, width_all)
    pseudo = scale_lines(summed, mode_freq, mode_damping, line_freq, columns)
    responses = jnp.dot(mode_rows, pseudo, preferred_element_type=jnp.float32).astype(jnp.bfloat16)
    rim_rows = boundary_rows.shape[0] // 2
    export = responses[boundary_rows]
    padded = extended(export, ((("region", "sub"), 0),), rim_rows)
    node_table = jnp.concatenate([padded[:rim_rows], responses, padded[3 * rim_rows :]], axis=0)
    stress = stress_coef[0][:, None] * node_table[connectivity[0]].astype(jnp.float32)
    for corner in range(1, connectivity.shape[0]):
        stress = stress + stress_coef[corner][:, None] * node_table[connectivity[corner]].astype(
            jnp.float32
        )
    squares = stress * stress
    power = jnp.stack(
        [
            jnp.mean(squares[:, line_no * columns : (line_no + 1) * columns], axis=1)
            for line_no in range(line_count)
        ],
        axis=0,
    )
    return power


def solution(mesh):
    placed = (
        P(("region", "sub"), None),
        P(("region", "sub"), None),
        P(("region", "sub"), None),
        P(),
        P(),
        P(),
        P(("region", "sub")),
        P(None, ("region", "sub")),
        P(None, ("region", "sub")),
    )
    return jax.shard_map(
        local, mesh=mesh, in_specs=placed, out_specs=P(None, ("region", "sub")), check_vma=False
    )
```

profile of v0, /device:TPU:24, one launch (start us, length us, event | category | flops | bytes accessed | tf_op | source)
XLA Modules:
  0.0 312.2 jit_solution(9872141562445316333)
XLA Ops:
  6.5 0.0 copy-start
  6.5 0.0 copy-start.5
  6.5 0.0 copy-start.6
  6.5 0.0 copy-start.3
  6.5 0.0 copy-start.4
  6.5 0.0 copy-start.1
  6.6 0.0 copy-start.2
  6.6 0.0 all-reduce.2.cloned.1.call-start
  6.6 0.6 copy-done
  7.3 2.4 fusion.14
  9.7 0.0 all-reduce.2.cloned.1.call-update
  9.7 0.0 copy-done.5
  9.7 0.6 fusion.13
  10.3 0.0 copy-done.6
  12.8 0.0 copy-done.3
  12.9 0.0 copy-done.4
  12.9 0.0 copy-done.1
  12.9 0.0 copy-done.2
  12.9 1.2 fusion.9
  14.2 262.5 %all-reduce.2.cloned.1.call-done = f32[4096,128]{0,1:T(8,128)} async-done(((f32[4096,128]{0,1:T(8,128)}), f32[4096,128]{0,1:T(8,128)}) %all-reduce.2.cloned.1.call-update) | async-done | bytes 2097168 | tf_op jit(solution)/shard_map/psum | solution.py:68
  276.7 1.8 subtract_convert_fusion.1
  278.5 3.7 %fusion = bf16[512,128]{0,1:T(8,128)(2,1)S(1)} fusion(bf16[512,4096]{1,0:T(8,128)(2,1)} %param.9, bf16[4096,32]{0,1:T(8,128)(2,1)S(1)} %get-tuple-element.11, bf16[4096,32]{0,1:T(8,128)(2,1)S(1)} %get-tuple-element.12, bf16[4096,32]{0,1:T(8,128)(2,1)S(1)} %get-tuple-element.8, bf16[4096,32]{0,1:T(8,128)(2,1)S(1)} %get-tuple-element.7), kind=kOutput, calls=%fused_computation.6 | convolution fusion | flops 541130752 | bytes 5373952 | tf_op jit(solution)/shard_map/dot_general | solution.py:72
  282.2 0.1 copy.25
  282.3 0.7 gather_fusion
  283.0 0.1 copy.34
  283.1 5.7 %collective-permute-start.1 = (bf16[64,128]{0,1:T(8,128)(2,1)S(1)}, bf16[64,128]{0,1:T(8,128)(2,1)S(1)}, u32[]{:S(2)}, u32[]{:S(2)}) collective-permute-start(bf16[64,128]{0,1:T(8,128)(2,1)S(1)} %copy.34), channel_id=1, source_target_pairs={{1,0},{2,1},{3,2},{4,3},{5,4},{6,5},{7,6},{8,7},{9,8},{10,9},{11,1... | collective-permute-start | bytes 49160 | tf_op jit(solution)/shard_map/ppermute | solution.py:17
  288.8 0.1 copy.33
  289.0 1.9 collective-permute-start
  290.9 0.0 collective-permute-done.1
  290.9 7.5 %collective-permute-done = bf16[64,128]{0,1:T(8,128)(2,1)S(1)} collective-permute-done((bf16[64,128]{0,1:T(8,128)(2,1)S(1)}, bf16[64,128]{0,1:T(8,128)(2,1)S(1)}, u32[]{:S(2)}, u32[]{:S(2)}) %collective-permute-start) | collective-permute-done | bytes 16416 | tf_op jit(solution)/shard_map/ppermute | solution.py:15
  298.4 0.1 pad_maximum_fusion
  298.5 0.2 copy.28
  298.7 1.3 gather_fusion.4
  300.1 1.3 gather_fusion.3
  301.4 1.3 gather_fusion.2
  302.7 1.3 gather_fusion.1
  304.1 0.3 add_multiply_fusion
  304.4 0.3 slice_reduce_fusion.1
  304.8 0.6 pad_maximum_fusion.1
  (10 shorter events, 0.1 us)
Async XLA Ops:
  6.5 0.7 copy-start
  6.5 3.2 %copy-start.5 = (f32[2]{0:T(128)S(1)}, f32[2]{0:T(128)}, u32[]{:S(2)}) copy-start(f32[2]{0:T(128)} %param.14) | copy-start | bytes 28
  6.5 3.8 %copy-start.6 = (s32[128]{0:T(128)S(1)}, s32[128]{0:T(128)}, u32[]{:S(2)}) copy-start(s32[128]{0:T(128)} %param.15) | copy-start | bytes 1540
  6.5 6.2 %copy-start.3 = (s32[4,512]{1,0:T(4,128)S(1)}, s32[4,512]{1,0:T(4,128)}, u32[]{:S(2)}) copy-start(s32[4,512]{1,0:T(4,128)} %param.16) | copy-start | bytes 24580
  6.5 6.3 %copy-start.4 = (f32[4,512]{1,0:T(4,128)S(1)}, f32[4,512]{1,0:T(4,128)}, u32[]{:S(2)}) copy-start(f32[4,512]{1,0:T(4,128)} %param.17) | copy-start | bytes 24580
  6.5 6.3 %copy-start.1 = (f32[4096]{0:T(1024)S(1)}, f32[4096]{0:T(1024)}, u32[]{:S(2)}) copy-start(f32[4096]{0:T(1024)} %param.12) | copy-start | bytes 49156
  6.6 6.3 %copy-start.2 = (f32[4096]{0:T(1024)S(1)}, f32[4096]{0:T(1024)}, u32[]{:S(2)}) copy-start(f32[4096]{0:T(1024)} %param.13) | copy-start | bytes 49156
  6.6 270.1 %all-reduce.2.cloned.1.call-start = ((), (), s32[]{:S(2)}) async-start(), calls=%async_computation | async-start | bytes 4194304 | tf_op jit(solution)/shard_map/psum | solution.py:68
  283.1 7.8 %collective-permute-start.1 = (bf16[64,128]{0,1:T(8,128)(2,1)S(1)}, bf16[64,128]{0,1:T(8,128)(2,1)S(1)}, u32[]{:S(2)}, u32[]{:S(2)}) collective-permute-start(bf16[64,128]{0,1:T(8,128)(2,1)S(1)} %copy.34), channel_id=1, source_target_pairs={{1,0},{2,1},{3,2},{4,3},{5,4},{6,5},{7,6},{8,7},{9,8},{10,9},{11,1... | collective-permute-start | bytes 49160 | tf_op jit(solution)/shard_map/ppermute | solution.py:17
  289.0 9.5 %collective-permute-start = (bf16[64,128]{0,1:T(8,128)(2,1)S(1)}, bf16[64,128]{0,1:T(8,128)(2,1)S(1)}, u32[]{:S(2)}, u32[]{:S(2)}) collective-permute-start(bf16[64,128]{0,1:T(8,128)(2,1)S(1)} %copy.33), channel_id=1, source_target_pairs={{0,1},{1,2},{2,3},{3,4},{4,5},{5,6},{6,7},{7,8},{8,9},{9,10},{10,1... | collective-permute-start | bytes 49160 | tf_op jit(solution)/shard_map/ppermute | solution.py:15
Sparse Core Ops, SparseCore 0:
  12.8 263.8 all-reduce.1
where the time goes:
time: 313 us; the launch traced here: 312 us
  waiting for transfers between devices  270 us (86%)
  between operations  16.1 us (5%)
  local copies, waits for them, and re-layouts  7.86 us (3%)
  starting transfers between devices  7.65 us (2%)
  matrix products  6.16 us (2%)
  other arithmetic  4.44 us (1%)
    psum x1, waiting for transfers between devices, local(): lax.psum(partial_value.reshape(mode_count // 2, 2 * width_all), ('region'...  263 us
    ppermute x1, waiting for transfers between devices, extended(): lax.ppermute(tail, axis, [(i, (i + 1) % count) for i in range(ends)])  7.5 us
  transfers between devices with their start and end apart: 3, of which 2 were waited for; matrix products, arithmetic and copies ran while one was open for 1% of the time, Pallas kernels for 0%

commit v1 on v0

v1 whole, which is shorter than its diff:
```python
import jax
import jax.numpy as jnp
from jax import lax
from jax.experimental import pallas as pl
from jax.experimental.pallas import tpu as pltpu
from jax.sharding import PartitionSpec as P

MESH = pl.DeviceIdType.MESH
NY, NZ, NX, NC = 4, 8, 4, 2
NPLANE = NY * NX * NC
DEVICES = NPLANE * NZ
LINES = 2
R = 32
BOUND = 64
F32 = jnp.float32
BF16 = jnp.bfloat16


def kernel(
    mode_hbm, rows_hbm, factor_hbm, freq_hbm, damp_hbm, line_hbm, brow_hbm, conn_hbm, coef_hbm,
    out_ref,
    modes, rows_v, factor_v, freq_v, damp_v, line_s, brow_v, conn_v, coef_v,
    r1, f1, r2, f2, pbuf, export, w_hi, w_lo, acc,
    load_sem, s1_send, s1_rrecv, s1_frecv, s2_send, s2_rrecv, s2_frecv,
    s3_send, s3_recv, s3_core, e_send, e_recv, own_sem,
):
    region = lax.axis_index("region")
    sub = lax.axis_index("sub")
    y, z = region // NZ, region % NZ
    x, c = sub // NC, sub % NC
    dev = region * (NX * NC) + sub
    q = (y * NX + x) * NC + c
    own = mode_hbm.shape[0]
    nodes = own + 2 * BOUND

    def device(yy, zz, xx, cc):
        return {"region": yy * NZ + zz, "sub": xx * NC + cc}

    plane = [(i, j, k) for i in range(NY) for j in range(NX) for k in range(NC)]
    plane = sorted(plane[1:], key=lambda o: -(min(o[0], NY - o[0]) + min(o[1], NX - o[1])))
    zs = [4, 3, 5, 2, 6, 1, 7]

    def plane_peer(o):
        yy, xx, cc = (y + o[0]) % NY, (x + o[1]) % NX, (c + o[2]) % NC
        return device(yy, z, xx, cc), (yy * NX + xx) * NC + cc

    nxt = (dev + 1) % DEVICES
    prv = (dev + DEVICES - 1) % DEVICES
    next_dev = {"region": nxt // (NX * NC), "sub": nxt % (NX * NC)}
    prev_dev = {"region": prv // (NX * NC), "sub": prv % (NX * NC)}

    loads = [
        pltpu.make_async_copy(rows_hbm, rows_v, load_sem.at[0]),
        pltpu.make_async_copy(factor_hbm, factor_v, load_sem.at[1]),
        pltpu.make_async_copy(conn_hbm, conn_v, load_sem.at[2]),
        pltpu.make_async_copy(coef_hbm, coef_v, load_sem.at[3]),
        pltpu.make_async_copy(mode_hbm, modes.at[pl.ds(BOUND, own)], load_sem.at[4]),
        pltpu.make_async_copy(brow_hbm, brow_v, load_sem.at[5]),
        pltpu.make_async_copy(freq_hbm, freq_v, load_sem.at[6]),
        pltpu.make_async_copy(damp_hbm, damp_v, load_sem.at[7]),
        pltpu.make_async_copy(line_hbm, line_s, load_sem.at[8]),
    ]
    for copy in loads:
        copy.start()

    barrier = pltpu.get_barrier_semaphore()
    greet = [plane_peer(o)[0] for o in plane]
    greet += [device(y, (z + k) % NZ, x, c) for k in zs]
    greet += [next_dev, prev_dev]
    for peer in greet:
        pl.semaphore_signal(barrier, inc=1, device_id=peer, device_id_type=MESH)

    for copy in loads[:4]:
        copy.wait()

    block = 64

    def build(step, carry):
        base = pl.multiple_of(step * block, block)
        node = base + lax.broadcasted_iota(jnp.int32, (block, conn_v.shape[1]), 0)
        total = jnp.zeros((block, conn_v.shape[1]), F32)
        for k in range(conn_v.shape[0]):
            total = total + jnp.where(node == conn_v[k : k + 1, :], coef_v[k : k + 1, :], 0.0)
        high = total.astype(BF16)
        w_hi[pl.ds(base, block), :] = high
        w_lo[pl.ds(base, block), :] = (total - high.astype(F32)).astype(BF16)
        return carry

    lax.fori_loop(0, nodes // block, build, 0)

    pl.semaphore_wait(barrier, len(greet))

    def remote(src, dst, send, recv, peer):
        return pltpu.make_async_remote_copy(
            src_ref=src, dst_ref=dst, send_sem=send, recv_sem=recv, device_id=peer, device_id_type=MESH
        )

    my_pair = r1.at[pl.ds(2 * q, 2)]
    for o in plane:
        peer, chunk = plane_peer(o)
        src = rows_v.at[:, pl.ds(pl.multiple_of(chunk * 128, 128), 128)]
        remote(src, my_pair, s1_send.at[0], s1_rrecv, peer).start()
    for k in zs:
        remote(factor_v, f1.at[z], s1_send.at[1], s1_frecv, device(y, (z + k) % NZ, x, c)).start()
    own_rows = pltpu.make_async_copy(
        rows_v.at[:, pl.ds(pl.multiple_of(q * 128, 128), 128)], my_pair, own_sem.at[0]
    )
    own_factor = pltpu.make_async_copy(factor_v, f1.at[z], own_sem.at[1])
    own_rows.start()
    own_factor.start()

    for copy in loads[4:]:
        copy.wait()
    picks = lax.broadcasted_iota(jnp.int32, (own, 2 * BOUND), 0) == brow_v[...]
    picks = jnp.where(picks, 1.0, 0.0).T.astype(BF16)
    width = 512

    def pick(step, carry):
        cols = pl.ds(pl.multiple_of(step * width, width), width)
        export[:, cols] = jnp.dot(
            picks, modes[pl.ds(BOUND, own), cols], preferred_element_type=F32
        ).astype(BF16)
        return carry

    lax.fori_loop(0, modes.shape[1] // width, pick, 0)

    own_rows.wait()
    own_factor.wait()
    got = r1.at[pl.ds(0, 2 * (NPLANE - 1))]
    pltpu.make_async_copy(got, got, s1_rrecv).wait()
    got = f1.at[pl.ds(0, NZ - 1)]
    pltpu.make_async_copy(got, got, s1_frecv).wait()

    for k in zs:
        remote(r1, r2.at[z], s2_send.at[0], s2_rrecv, device(y, (z + k) % NZ, x, c)).start()
    for o in plane:
        remote(f1, f2.at[:, q], s2_send.at[1], s2_frecv, plane_peer(o)[0]).start()
    own_rows = pltpu.make_async_copy(r1, r2.at[z], own_sem.at[0])
    own_factor = pltpu.make_async_copy(f1, f2.at[:, q], own_sem.at[1])
    own_rows.start()
    own_factor.start()

    to_prev = remote(
        export.at[pl.ds(0, BOUND)], modes.at[pl.ds(own + BOUND, BOUND)], e_send.at[0], e_recv.at[0], prev_dev
    )
    to_next = remote(
        export.at[pl.ds(BOUND, BOUND)], modes.at[pl.ds(0, BOUND)], e_send.at[1], e_recv.at[1], next_dev
    )
    to_prev.start()
    to_next.start()

    freq = freq_v[pl.ds(q, 1), :]
    damp = damp_v[pl.ds(q, 1), :]
    gains = []
    for line in range(LINES):
        omega = line_s[line]
        detune = freq * freq - omega * omega
        damped = 2.0 * damp * freq * omega
        magnitude = detune * detune + damped * damped
        gains.append((detune / magnitude, -damped / magnitude))

    own_rows.wait()
    own_factor.wait()
    got = r2.at[pl.ds(0, NZ - 1)]
    pltpu.make_async_copy(got, got, s2_rrecv).wait()
    got = f2.at[:, pl.ds(0, NPLANE - 1)]
    pltpu.make_async_copy(got, got, s2_frecv).wait()

    inputs = NZ * NPLANE * 2
    forced = lax.dot_general(
        f2.reshape(inputs, 128)[...], r2.reshape(inputs, 128)[...],
        (((0,), (0,)), ((), ())), preferred_element_type=F32,
    )
    parts = []
    for line in range(LINES):
        real = forced[line * 2 * R : line * 2 * R + R]
        imag = forced[line * 2 * R + R : (line + 1) * 2 * R]
        gain_real, gain_imag = gains[line]
        parts.append(gain_real * real - gain_imag * imag)
        parts.append(gain_real * imag + gain_imag * real)
    pbuf[pl.ds(pl.multiple_of(q * 128, 128), 128), :] = jnp.concatenate(parts, axis=0).T.astype(BF16)

    grid = [(i, j) for i in range(NY) for j in range(NX)]
    near = sorted(grid, key=lambda o: min(o[0], NY - o[0]) + min(o[1], NX - o[1]))
    core_peer = device(y, z, x, 1 - c)

    def chunk_rows(pair, core):
        return pl.ds(pl.multiple_of((pair * NC + core) * 128, 128), 128)

    mine = pbuf.at[chunk_rows(y * NX + x, c)]
    for i, j in reversed(near[1:]):
        peer = device((y + i) % NY, z, (x + j) % NX, c)
        remote(mine, mine, s3_send, s3_recv.at[i * NX + j], peer).start()

    def source(o):
        return ((y + NY - o[0]) % NY) * NX + (x + NX - o[1]) % NX

    def add(o, first):
        pair = source(o)
        landed = pbuf.at[chunk_rows(pair, 1 - c)]
        pltpu.make_async_copy(landed, landed, s3_core.at[o[0] * NX + o[1]]).wait()
        span = pl.ds(pl.multiple_of(pair * 256, 256), 256)
        term = jnp.dot(modes[:, span], pbuf[span, :], preferred_element_type=F32)
        acc[...] = term if first else acc[...] + term

    before = None
    for n, o in enumerate(near):
        piece = pbuf.at[chunk_rows(source(o), c)]
        if n:
            pltpu.make_async_copy(piece, piece, s3_recv.at[o[0] * NX + o[1]]).wait()
        remote(piece, piece, s3_send, s3_core.at[o[0] * NX + o[1]], core_peer).start()
        if n == 0:
            to_prev.wait_recv()
            to_next.wait_recv()
        if before is not None:
            add(before, n == 1)
        before = o
    add(before, False)

    responses = acc[...]
    lower = jnp.where(dev > 0, responses[:BOUND], 0.0)
    upper = jnp.where(dev < DEVICES - 1, responses[own + BOUND :], 0.0)
    table = jnp.concatenate([lower, responses[BOUND : own + BOUND], upper], axis=0)
    table = table.T.astype(BF16)
    stress = jnp.dot(table, w_hi[...], preferred_element_type=F32)
    stress = stress + jnp.dot(table, w_lo[...], preferred_element_type=F32)
    squares = stress * stress
    for line in range(LINES):
        part = squares[line * 2 * R : (line + 1) * 2 * R]
        out_ref[line : line + 1, :] = jnp.sum(part, axis=0, keepdims=True) * (1.0 / (2 * R))

    got = r1.at[pl.ds(0, 2 * (NPLANE - 1))]
    pltpu.make_async_copy(got, got, s1_send.at[0]).wait()
    got = f1.at[pl.ds(0, NZ - 1)]
    pltpu.make_async_copy(got, got, s1_send.at[1]).wait()
    got = r2.at[pl.ds(0, NZ - 1)]
    pltpu.make_async_copy(got, got, s2_send.at[0]).wait()
    got = f2.at[:, pl.ds(0, NPLANE - 1)]
    pltpu.make_async_copy(got, got, s2_send.at[1]).wait()
    got = pbuf.at[pl.ds(0, 128 * (2 * NY * NX - 1))]
    pltpu.make_async_copy(got, got, s3_send).wait()
    to_prev.wait_send()
    to_next.wait_send()


def local(
    mode_rows, input_rows, input_factor, mode_freq, mode_damping, line_freq, boundary_rows, connectivity,
    stress_coef,
):
    own, modes = mode_rows.shape
    nodes = own + 2 * BOUND
    elements = connectivity.shape[1]
    dma = pltpu.SemaphoreType.DMA
    return pl.pallas_call(
        kernel,
        name="modal_stress",
        out_shape=jax.ShapeDtypeStruct((LINES, elements), F32),
        in_specs=[pl.BlockSpec(memory_space=pl.ANY)] * 9,
        out_specs=pl.BlockSpec(memory_space=pltpu.VMEM),
        scratch_shapes=[
            pltpu.VMEM((nodes, modes), BF16),
            pltpu.VMEM((2, modes), BF16),
            pltpu.VMEM((2, 128), BF16),
            pltpu.VMEM((NPLANE, 128), F32),
            pltpu.VMEM((NPLANE, 128), F32),
            pltpu.SMEM((LINES,), F32),
            pltpu.VMEM((1, 2 * BOUND), jnp.int32),
            pltpu.VMEM(connectivity.shape, jnp.int32),
            pltpu.VMEM(stress_coef.shape, F32),
            pltpu.VMEM((2 * NPLANE, 128), BF16),
            pltpu.VMEM((NZ, 2, 128), BF16),
            pltpu.VMEM((NZ, 2 * NPLANE, 128), BF16),
            pltpu.VMEM((NZ, NPLANE, 2, 128), BF16),
            pltpu.VMEM((modes, 128), BF16),
            pltpu.VMEM((2 * BOUND, modes), BF16),
            pltpu.VMEM((nodes, elements), BF16),
            pltpu.VMEM((nodes, elements), BF16),
            pltpu.VMEM((nodes, 128), F32),
            dma((9,)),
            dma((2,)),
            dma(()),
            dma(()),
            dma((2,)),
            dma(()),
            dma(()),
            dma(()),
            dma((NY * NX,)),
            dma((NY * NX,)),
            dma((2,)),
            dma((2,)),
            dma((2,)),
        ],
        compiler_params=pltpu.CompilerParams(
            collective_id=0, has_side_effects=True, vmem_limit_bytes=48 << 20
        ),
    )(
        mode_rows,
        input_rows,
        input_factor,
        mode_freq.reshape(NPLANE, 128),
        mode_damping.reshape(NPLANE, 128),
        line_freq,
        boundary_rows.reshape(1, 2 * BOUND),
        connectivity,
        stress_coef,
    )


def solution(mesh):
    split = ("region", "sub")
    placed = (
        P(split, None),
        P(split, None),
        P(split, None),
        P(),
        P(),
        P(),
        P(split),
        P(None, split),
        P(None, split),
    )
    return jax.shard_map(
        local, mesh=mesh, in_specs=placed, out_specs=P(None, split), check_vma=False
    )
```

time: 313 us -> 52.3 us (0.17)
  the two profiles are of different devices: /device:TPU:24 before, /device:TPU:1 now
where the time goes in v1:
time: 52.3 us; the launch traced here: 51.8 us
  Pallas kernels  43.5 us (83%)
  local copies, waits for them, and re-layouts  8.29 us (16%)
    pallas_call x1, Pallas kernels, local(): pl.pallas_call(kernel, name='modal_stress', out_shape=jax.ShapeDtypeStruc...  43.5 us
    unnamed x19, local copies, waits for them, and re-layouts  8.29 us

profile of v1, /device:TPU:1, one launch (start us, length us, event | category | flops | bytes accessed | tf_op | source)
XLA Modules:
  0.0 51.8 jit_solution(12032333358154245585)
XLA Ops:
  0.0 0.0 copy-start
  0.0 2.2 %copy-done = bf16[512,4096]{1,0:T(8,128)(2,1)S(1)} copy-done((bf16[512,4096]{1,0:T(8,128)(2,1)S(1)}, bf16[512,4096]{1,0:T(8,128)(2,1)}, u32[]{:S(2)}) %copy-start) | copy-done | bytes 4194328
  2.2 0.0 copy-start.1
  2.2 0.7 %copy-done.1 = bf16[2,4096]{1,0:T(2,128)(2,1)S(1)} copy-done((bf16[2,4096]{1,0:T(2,128)(2,1)S(1)}, bf16[2,4096]{1,0:T(2,128)(2,1)}, u32[]{:S(2)}) %copy-start.1) | copy-done | bytes 16408
  2.9 0.0 copy-start.2
  2.9 0.7 %copy-done.2 = f32[4096]{0:T(1024)S(1)} copy-done((f32[4096]{0:T(1024)S(1)}, f32[4096]{0:T(1024)}, u32[]{:S(2)}) %copy-start.2) | copy-done | bytes 16408
  3.6 0.0 copy-start.3
  3.6 0.7 %copy-done.3 = f32[4096]{0:T(1024)S(1)} copy-done((f32[4096]{0:T(1024)S(1)}, f32[4096]{0:T(1024)}, u32[]{:S(2)}) %copy-start.3) | copy-done | bytes 16408
  4.3 0.0 copy-start.4
  4.3 0.7 %copy-done.4 = s32[4,512]{1,0:T(4,128)S(1)} copy-done((s32[4,512]{1,0:T(4,128)S(1)}, s32[4,512]{1,0:T(4,128)}, u32[]{:S(2)}) %copy-start.4) | copy-done | bytes 8216
  5.0 0.0 copy-start.5
  5.0 0.7 %copy-done.5 = f32[4,512]{1,0:T(4,128)S(1)} copy-done((f32[4,512]{1,0:T(4,128)S(1)}, f32[4,512]{1,0:T(4,128)}, u32[]{:S(2)}) %copy-start.5) | copy-done | bytes 8216
  5.7 0.0 copy-start.6
  5.7 0.7 %copy-done.6 = bf16[2,128]{1,0:T(2,128)(2,1)S(1)} copy-done((bf16[2,128]{1,0:T(2,128)(2,1)S(1)}, bf16[2,128]{1,0:T(2,128)(2,1)}, u32[]{:S(2)}) %copy-start.6) | copy-done | bytes 536
  6.4 0.0 copy-start.7
  6.4 0.7 %copy-done.7 = f32[2]{0:T(128)S(1)} copy-done((f32[2]{0:T(128)S(1)}, f32[2]{0:T(128)}, u32[]{:S(2)}) %copy-start.7) | copy-done | bytes 32
  7.0 0.0 copy-start.8
  7.1 0.7 %copy-done.8 = s32[128]{0:T(128)S(1)} copy-done((s32[128]{0:T(128)S(1)}, s32[128]{0:T(128)}, u32[]{:S(2)}) %copy-start.8) | copy-done | bytes 536
  7.7 43.5 %modal_stress.1 = f32[2,512]{1,0:T(2,128)S(1)} custom-call(bf16[512,4096]{1,0:T(8,128)(2,1)S(1)} %copy-done, bf16[2,4096]{1,0:T(2,128)(2,1)S(1)} %copy-done.1, bf16[2,128]{1,0:T(2,128)(2,1)S(1)} %copy-done.6, f32[32,128]{1,0:T(8,128)S(1)} %bitcast.3, f32[32,128]{1,0:T(8,128)S(1)} %bitcast.4, f32[2]{0:T(128)S(1)} %copy-done.7, s32[1,128]{1,0:T(1,128)S(1)} %bitcast.5, ...), custom_call_target="tpu_custom_call" | custom-call | tf_op jit(solution)/shard_map/modal_stress/pallas_call | solution.py:254
  51.3 0.6 %copy.11 = f32[2,512]{1,0:T(2,128)} copy(f32[2,512]{1,0:T(2,128)S(1)} %modal_stress.1) | data formatting | bytes 8192
Async XLA Ops:
  0.0 2.2 %copy-start = (bf16[512,4096]{1,0:T(8,128)(2,1)S(1)}, bf16[512,4096]{1,0:T(8,128)(2,1)}, u32[]{:S(2)}) copy-start(bf16[512,4096]{1,0:T(8,128)(2,1)} %mode_hbm.1) | copy-start | bytes 12582916
  2.2 0.7 %copy-start.1 = (bf16[2,4096]{1,0:T(2,128)(2,1)S(1)}, bf16[2,4096]{1,0:T(2,128)(2,1)}, u32[]{:S(2)}) copy-start(bf16[2,4096]{1,0:T(2,128)(2,1)} %rows_hbm.1) | copy-start | bytes 49156
  2.9 0.7 %copy-start.2 = (f32[4096]{0:T(1024)S(1)}, f32[4096]{0:T(1024)}, u32[]{:S(2)}) copy-start(f32[4096]{0:T(1024)} %param.12) | copy-start | bytes 49156
  3.6 0.7 %copy-start.3 = (f32[4096]{0:T(1024)S(1)}, f32[4096]{0:T(1024)}, u32[]{:S(2)}) copy-start(f32[4096]{0:T(1024)} %param.13) | copy-start | bytes 49156
  4.3 0.7 %copy-start.4 = (s32[4,512]{1,0:T(4,128)S(1)}, s32[4,512]{1,0:T(4,128)}, u32[]{:S(2)}) copy-start(s32[4,512]{1,0:T(4,128)} %conn_hbm.1) | copy-start | bytes 24580
  5.0 0.7 %copy-start.5 = (f32[4,512]{1,0:T(4,128)S(1)}, f32[4,512]{1,0:T(4,128)}, u32[]{:S(2)}) copy-start(f32[4,512]{1,0:T(4,128)} %coef_hbm.1) | copy-start | bytes 24580
  5.7 0.7 %copy-start.6 = (bf16[2,128]{1,0:T(2,128)(2,1)S(1)}, bf16[2,128]{1,0:T(2,128)(2,1)}, u32[]{:S(2)}) copy-start(bf16[2,128]{1,0:T(2,128)(2,1)} %factor_hbm.1) | copy-start | bytes 1540
  6.4 0.7 %copy-start.7 = (f32[2]{0:T(128)S(1)}, f32[2]{0:T(128)}, u32[]{:S(2)}) copy-start(f32[2]{0:T(128)} %line_hbm.1) | copy-start | bytes 28
  7.0 0.7 %copy-start.8 = (s32[128]{0:T(128)S(1)}, s32[128]{0:T(128)}, u32[]{:S(2)}) copy-start(s32[128]{0:T(128)} %param.15) | copy-start | bytes 1540

commit v2 on v1

--- a/solution.py
+++ b/solution.py
@@ -12,6 +12,7 @@
 LINES = 2
 R = 32
 BOUND = 64
+LAG = 3
 F32 = jnp.float32
 BF16 = jnp.bfloat16
 
@@ -29,7 +30,7 @@
     y, z = region // NZ, region % NZ
     x, c = sub // NC, sub % NC
     dev = region * (NX * NC) + sub
-    q = (y * NX + x) * NC + c
+    q = (c * NY + y) * NX + x
     own = mode_hbm.shape[0]
     nodes = own + 2 * BOUND
 
@@ -42,7 +43,7 @@
 
     def plane_peer(o):
         yy, xx, cc = (y + o[0]) % NY, (x + o[1]) % NX, (c + o[2]) % NC
-        return device(yy, z, xx, cc), (yy * NX + xx) * NC + cc
+        return device(yy, z, xx, cc), (cc * NY + yy) * NX + xx
 
     nxt = (dev + 1) % DEVICES
     prv = (dev + DEVICES - 1) % DEVICES
@@ -50,12 +51,12 @@
     prev_dev = {"region": prv // (NX * NC), "sub": prv % (NX * NC)}
 
     loads = [
+        pltpu.make_async_copy(mode_hbm, modes.at[pl.ds(BOUND, own)], load_sem.at[4]),
+        pltpu.make_async_copy(brow_hbm, brow_v, load_sem.at[5]),
         pltpu.make_async_copy(rows_hbm, rows_v, load_sem.at[0]),
         pltpu.make_async_copy(factor_hbm, factor_v, load_sem.at[1]),
         pltpu.make_async_copy(conn_hbm, conn_v, load_sem.at[2]),
         pltpu.make_async_copy(coef_hbm, coef_v, load_sem.at[3]),
-        pltpu.make_async_copy(mode_hbm, modes.at[pl.ds(BOUND, own)], load_sem.at[4]),
-        pltpu.make_async_copy(brow_hbm, brow_v, load_sem.at[5]),
         pltpu.make_async_copy(freq_hbm, freq_v, load_sem.at[6]),
         pltpu.make_async_copy(damp_hbm, damp_v, load_sem.at[7]),
         pltpu.make_async_copy(line_hbm, line_s, load_sem.at[8]),
@@ -64,13 +65,69 @@
         copy.start()
 
     barrier = pltpu.get_barrier_semaphore()
-    greet = [plane_peer(o)[0] for o in plane]
-    greet += [device(y, (z + k) % NZ, x, c) for k in zs]
+    greet = [device(y, (z + k) % NZ, x, c) for k in zs[:3]]
+    greet += [plane_peer(o)[0] for o in plane[:8]]
     greet += [next_dev, prev_dev]
+    greet += [device(y, (z + k) % NZ, x, c) for k in zs[3:]]
+    greet += [plane_peer(o)[0] for o in plane[8:]]
     for peer in greet:
         pl.semaphore_signal(barrier, inc=1, device_id=peer, device_id_type=MESH)
 
     for copy in loads[:4]:
+        copy.wait()
+    picks = lax.broadcasted_iota(jnp.int32, (own, 2 * BOUND), 0) == brow_v[...]
+    picks = jnp.where(picks, 1.0, 0.0).T.astype(BF16)
+    width = 512
+
+    def pick(step, carry):
+        cols = pl.ds(pl.multiple_of(step * width, width), width)
+        export[:, cols] = jnp.dot(
+            picks, modes[pl.ds(BOUND, own), cols], preferred_element_type=F32
+        ).astype(BF16)
+        return carry
+
+    lax.fori_loop(0, modes.shape[1] // width, pick, 0)
+
+    pl.semaphore_wait(barrier, len(greet))
+
+    def remote(src, dst, send, recv, peer):
+        return pltpu.make_async_remote_copy(
+            src_ref=src, dst_ref=dst, send_sem=send, recv_sem=recv, device_id=peer, device_id_type=MESH
+        )
+
+    pending = []
+
+    def drain(part, sem):
+        pending.append(pltpu.make_async_copy(part, part, sem).wait)
+
+    for k in zs:
+        remote(factor_v, f1.at[z], s1_send.at[1], s1_frecv, device(y, (z + k) % NZ, x, c)).start()
+    my_pair = r1.at[pl.ds(2 * q, 2)]
+    for o in plane:
+        peer, chunk = plane_peer(o)
+        src = rows_v.at[:, pl.ds(pl.multiple_of(chunk * 128, 128), 128)]
+        remote(src, my_pair, s1_send.at[0], s1_rrecv, peer).start()
+    own_rows = pltpu.make_async_copy(
+        rows_v.at[:, pl.ds(pl.multiple_of(q * 128, 128), 128)], my_pair, own_sem.at[0]
+    )
+    own_factor = pltpu.make_async_copy(factor_v, f1.at[z], own_sem.at[1])
+    own_rows.start()
+    own_factor.start()
+    drain(r1.at[pl.ds(0, 2 * (NPLANE - 1))], s1_send.at[0])
+    drain(f1.at[pl.ds(0, NZ - 1)], s1_send.at[1])
+
+    to_prev = remote(
+        export.at[pl.ds(0, BOUND)], modes.at[pl.ds(own + BOUND, BOUND)], e_send.at[0], e_recv.at[0], prev_dev
+    )
+    to_next = remote(
+        export.at[pl.ds(BOUND, BOUND)], modes.at[pl.ds(0, BOUND)], e_send.at[1], e_recv.at[1], next_dev
+    )
+    to_prev.start()
+    to_next.start()
+    pending.append(to_prev.wait_send)
+    pending.append(to_next.wait_send)
+
+    for copy in loads[4:]:
         copy.wait()
 
     block = 64
@@ -88,66 +145,23 @@
 
     lax.fori_loop(0, nodes // block, build, 0)
 
-    pl.semaphore_wait(barrier, len(greet))
-
-    def remote(src, dst, send, recv, peer):
-        return pltpu.make_async_remote_copy(
-            src_ref=src, dst_ref=dst, send_sem=send, recv_sem=recv, device_id=peer, device_id_type=MESH
-        )
-
-    my_pair = r1.at[pl.ds(2 * q, 2)]
+    own_factor.wait()
+    got = f1.at[pl.ds(0, NZ - 1)]
+    pltpu.make_async_copy(got, got, s1_frecv).wait()
     for o in plane:
-        peer, chunk = plane_peer(o)
-        src = rows_v.at[:, pl.ds(pl.multiple_of(chunk * 128, 128), 128)]
-        remote(src, my_pair, s1_send.at[0], s1_rrecv, peer).start()
-    for k in zs:
-        remote(factor_v, f1.at[z], s1_send.at[1], s1_frecv, device(y, (z + k) % NZ, x, c)).start()
-    own_rows = pltpu.make_async_copy(
-        rows_v.at[:, pl.ds(pl.multiple_of(q * 128, 128), 128)], my_pair, own_sem.at[0]
-    )
-    own_factor = pltpu.make_async_copy(factor_v, f1.at[z], own_sem.at[1])
-    own_rows.start()
+        remote(f1, f2.at[:, q], s2_send.at[1], s2_frecv, plane_peer(o)[0]).start()
+    own_factor = pltpu.make_async_copy(f1, f2.at[:, q], own_sem.at[1])
     own_factor.start()
-
-    for copy in loads[4:]:
-        copy.wait()
-    picks = lax.broadcasted_iota(jnp.int32, (own, 2 * BOUND), 0) == brow_v[...]
-    picks = jnp.where(picks, 1.0, 0.0).T.astype(BF16)
-    width = 512
-
-    def pick(step, carry):
-        cols = pl.ds(pl.multiple_of(step * width, width), width)
-        export[:, cols] = jnp.dot(
-            picks, modes[pl.ds(BOUND, own), cols], preferred_element_type=F32
-        ).astype(BF16)
-        return carry
-
-    lax.fori_loop(0, modes.shape[1] // width, pick, 0)
+    drain(f2.at[:, pl.ds(0, NPLANE - 1)], s2_send.at[1])
 
     own_rows.wait()
-    own_factor.wait()
     got = r1.at[pl.ds(0, 2 * (NPLANE - 1))]
     pltpu.make_async_copy(got, got, s1_rrecv).wait()
-    got = f1.at[pl.ds(0, NZ - 1)]
-    pltpu.make_async_copy(got, got, s1_frecv).wait()
-
     for k in zs:
         remote(r1, r2.at[z], s2_send.at[0], s2_rrecv, device(y, (z + k) % NZ, x, c)).start()
-    for o in plane:
-        remote(f1, f2.at[:, q], s2_send.at[1], s2_frecv, plane_peer(o)[0]).start()
     own_rows = pltpu.make_async_copy(r1, r2.at[z], own_sem.at[0])
-    own_factor = pltpu.make_async_copy(f1, f2.at[:, q], own_sem.at[1])
     own_rows.start()
-    own_factor.start()
-
-    to_prev = remote(
-        export.at[pl.ds(0, BOUND)], modes.at[pl.ds(own + BOUND, BOUND)], e_send.at[0], e_recv.at[0], prev_dev
-    )
-    to_next = remote(
-        export.at[pl.ds(BOUND, BOUND)], modes.at[pl.ds(0, BOUND)], e_send.at[1], e_recv.at[1], next_dev
-    )
-    to_prev.start()
-    to_next.start()
+    drain(r2.at[pl.ds(0, NZ - 1)], s2_send.at[0])
 
     freq = freq_v[pl.ds(q, 1), :]
     damp = damp_v[pl.ds(q, 1), :]
@@ -180,42 +194,50 @@
         parts.append(gain_real * imag + gain_imag * real)
     pbuf[pl.ds(pl.multiple_of(q * 128, 128), 128), :] = jnp.concatenate(parts, axis=0).T.astype(BF16)
 
-    grid = [(i, j) for i in range(NY) for j in range(NX)]
-    near = sorted(grid, key=lambda o: min(o[0], NY - o[0]) + min(o[1], NX - o[1]))
+    def flip(v, bits):
+        return (v, v + 1 - 2 * (v % 2), (v + 2) % 4, 3 - v)[bits]
+
+    hops = (0, 1, 2, 1)
+    offsets = [(i, j) for i in range(NY) for j in range(NX)]
+    mine = pbuf.at[pl.ds(pl.multiple_of(q * 128, 128), 128)]
+    for i, j in sorted(offsets[1:], key=lambda o: -hops[o[0]] - hops[o[1]]):
+        peer = device(flip(y, i), z, flip(x, j), c)
+        remote(mine, mine, s3_send, s3_recv.at[i * NX + j], peer).start()
+
     core_peer = device(y, z, x, 1 - c)
-
-    def chunk_rows(pair, core):
-        return pl.ds(pl.multiple_of((pair * NC + core) * 128, 128), 128)
-
-    mine = pbuf.at[chunk_rows(y * NX + x, c)]
-    for i, j in reversed(near[1:]):
-        peer = device((y + i) % NY, z, (x + j) % NX, c)
-        remote(mine, mine, s3_send, s3_recv.at[i * NX + j], peer).start()
-
-    def source(o):
-        return ((y + NY - o[0]) % NY) * NX + (x + NX - o[1]) % NX
-
-    def add(o, first):
-        pair = source(o)
-        landed = pbuf.at[chunk_rows(pair, 1 - c)]
-        pltpu.make_async_copy(landed, landed, s3_core.at[o[0] * NX + o[1]]).wait()
-        span = pl.ds(pl.multiple_of(pair * 256, 256), 256)
-        term = jnp.dot(modes[:, span], pbuf[span, :], preferred_element_type=F32)
+    pairs = [(i, h) for i in range(NY) for h in range(2)]
+    pairs = sorted(pairs, key=lambda p: hops[p[0]] + p[1])
+
+    def span(pair, core):
+        i, h = pair
+        half = x // 2 if h == 0 else 1 - x // 2
+        return pl.ds(pl.multiple_of(((core * NY + flip(y, i)) * NX + 2 * half) * 128, 256), 256)
+
+    def add(rows, first=False):
+        term = jnp.dot(modes[:, rows], pbuf[rows, :], preferred_element_type=F32)
         acc[...] = term if first else acc[...] + term
 
-    before = None
-    for n, o in enumerate(near):
-        piece = pbuf.at[chunk_rows(source(o), c)]
-        if n:
-            pltpu.make_async_copy(piece, piece, s3_recv.at[o[0] * NX + o[1]]).wait()
-        remote(piece, piece, s3_send, s3_core.at[o[0] * NX + o[1]], core_peer).start()
+    def add_other(pair):
+        rows = span(pair, 1 - c)
+        landed = pbuf.at[rows]
+        pltpu.make_async_copy(landed, landed, s3_core.at[pair[0] * 2 + pair[1]]).wait()
+        add(rows)
+
+    for n, pair in enumerate(pairs):
+        rows = span(pair, c)
+        piece = pbuf.at[rows]
+        for j in (2 * pair[1], 2 * pair[1] + 1):
+            if (pair[0], j) != (0, 0):
+                pltpu.make_async_copy(mine, mine, s3_recv.at[pair[0] * NX + j]).wait()
+        remote(piece, piece, s3_send, s3_core.at[pair[0] * 2 + pair[1]], core_peer).start()
         if n == 0:
             to_prev.wait_recv()
             to_next.wait_recv()
-        if before is not None:
-            add(before, n == 1)
-        before = o
-    add(before, False)
+        add(rows, n == 0)
+        if n >= LAG:
+            add_other(pairs[n - LAG])
+    for pair in pairs[len(pairs) - LAG :]:
+        add_other(pair)
 
     responses = acc[...]
     lower = jnp.where(dev > 0, responses[:BOUND], 0.0)
@@ -229,18 +251,9 @@
         part = squares[line * 2 * R : (line + 1) * 2 * R]
         out_ref[line : line + 1, :] = jnp.sum(part, axis=0, keepdims=True) * (1.0 / (2 * R))
 
-    got = r1.at[pl.ds(0, 2 * (NPLANE - 1))]
-    pltpu.make_async_copy(got, got, s1_send.at[0]).wait()
-    got = f1.at[pl.ds(0, NZ - 1)]
-    pltpu.make_async_copy(got, got, s1_send.at[1]).wait()
-    got = r2.at[pl.ds(0, NZ - 1)]
-    pltpu.make_async_copy(got, got, s2_send.at[0]).wait()
-    got = f2.at[:, pl.ds(0, NPLANE - 1)]
-    pltpu.make_async_copy(got, got, s2_send.at[1]).wait()
-    got = pbuf.at[pl.ds(0, 128 * (2 * NY * NX - 1))]
-    pltpu.make_async_copy(got, got, s3_send).wait()
-    to_prev.wait_send()
-    to_next.wait_send()
+    drain(pbuf.at[pl.ds(0, 128 * (2 * NY * NX - 1))], s3_send)
+    for wait in pending:
+        wait()
 
 
 def local(
@@ -285,13 +298,13 @@
             dma(()),
             dma(()),
             dma((NY * NX,)),
-            dma((NY * NX,)),
+            dma((NY * 2,)),
             dma((2,)),
             dma((2,)),
             dma((2,)),
         ],
         compiler_params=pltpu.CompilerParams(
-            collective_id=0, has_side_effects=True, vmem_limit_bytes=48 << 20
+            collective_id=0, has_side_effects=True, vmem_limit_bytes=62 << 20
         ),
     )(
         mode_rows,

time: 52.3 us -> 37.5 us (0.72)
  Pallas kernels: 43.5 us -> 36.1 us
  local copies, waits for them, and re-layouts: 8.29 us -> 1.28 us
    pallas_call x1, Pallas kernels: 43.5 us -> 36.1 us  [local(): pl.pallas_call(kernel, name='modal_stress', out_shape=jax.ShapeDtypeStruc...]
    unnamed x19 -> x1, local copies, waits for them, and re-layouts: 8.29 us -> 1.28 us
where the time goes in v2:
time: 37.5 us; the launch traced here: 37.4 us
  Pallas kernels  36.1 us (96%)
  local copies, waits for them, and re-layouts  1.28 us (3%)
    pallas_call x1, Pallas kernels, local(): pl.pallas_call(kernel, name='modal_stress', out_shape=jax.ShapeDtypeStruc...  36.1 us
    unnamed x1, local copies, waits for them, and re-layouts  1.28 us

profile of v2, /device:TPU:1, one launch (start us, length us, event | category | flops | bytes accessed | tf_op | source)
XLA Modules:
  0.0 37.4 jit_solution(8702549769372375866)
XLA Ops:
  0.0 36.1 %modal_stress.1 = f32[2,512]{1,0:T(2,128)} custom-call(bf16[512,4096]{1,0:T(8,128)(2,1)} %mode_hbm.1, bf16[2,4096]{1,0:T(2,128)(2,1)} %rows_hbm.1, bf16[2,128]{1,0:T(2,128)(2,1)} %factor_hbm.1, f32[32,128]{1,0:T(8,128)} %bitcast.3, f32[32,128]{1,0:T(8,128)} %bitcast.4, f32[2]{0:T(128)} %line_hbm.1, s32[1,128]{1,0:T(1,128)} %bitcast.5, s32[4,512]{1,0:T(4,128)} %conn_hbm.1, ...), custom_call_target="tpu_custom_call" | custom-call | tf_op jit(solution)/shard_map/modal_stress/pallas_call | solution.py:267
  36.1 1.3 %copy.11 = f32[2,512]{1,0:T(2,128)} copy(f32[2,512]{1,0:T(2,128)} %modal_stress.1) | data formatting | bytes 8192
